TPU v7x, 256 devices: a whole 4x4x8 slice. The times are simulated.
256 devices in a mesh: dp: 32 (over x, z), seq: 8 (over y, core).
Axes of the slice: x: 4, y: 4, z: 8, core: 2. Of those that a mesh axis runs over, the one named last changes fastest.
Arguments:
- span_store: bfloat16 [32, 512, 8192], P('dp', 'seq'), may hold values from -6 to 6
- target: int32 [32, 512], P('dp', 'seq'), may hold values from 0 to 31, as said below
- segment_ids: int32 [32, 512], P('dp'), may hold values from 0 to 7, never falling along the last dimension, each value on 1 to 128 neighbouring positions
- norm_gain: float32 [8192], replicated, may hold values from 0.25 to 1.75
- w_query: bfloat16 [8192, 4096], P('dp', 'seq'), may hold values from -0.0625 to 0.0625
- key_weight: bfloat16 [8192, 1024], P('dp', 'seq'), may hold values from -0.0625 to 0.0625
- value_weight: bfloat16 [8192, 1024], P('dp', 'seq'), may hold values from -0.0625 to 0.0625
Outputs:
- context: bfloat16 [32, 512, 4096], P('dp', 'seq')
Inputs may be any that keep to these rules, and one draw needn't show every extreme that they name: `target`: within one lane, the stored tokens of all shards that name one packed row number exactly 64; one shard's tokens of one lane name one row at most 3 times, and exactly 3 times for some shard and row in every lane. `segment_ids`: along a row, document ids never fall.
All inputs are finite; a program needn't handle non-finite values.
Results may differ from a plain program's by a relative error of at most 0.0079.
Values may be sent and summed in bfloat16 or wider, within the bound.
No kernel may reach another device: no remote copies, remote signals or barrier semaphores. Data moves between devices by JAX's collectives and lax.ppermute only.
A program may use at most 128 MiB of HBM per device.

v0:
```python
import jax
import jax.numpy as jnp
from jax import lax
from jax.sharding import PartitionSpec as P

HEAD_SIZE = 128
epsilon = 1e-05
rope_base = 500000.0


def rotary_angles(values, token_positions):
    half_dim = values.shape[-1] // 2
    exponent = jnp.arange(half_dim, dtype=jnp.float32) * (2.0 / values.shape[-1])
    frequency = rope_base ** (-exponent)
    angles = token_positions.astype(jnp.float32)[:, None] * frequency[None, :]
    cosine = jnp.concatenate([jnp.cos(angles), jnp.cos(angles)], axis=-1)[:, None, :]
    sine_part = jnp.concatenate([jnp.sin(angles), jnp.sin(angles)], axis=-1)[:, None, :]
    rotated = jnp.concatenate([-values[..., half_dim:], values[..., :half_dim]], axis=-1)
    return values * cosine + rotated * sine_part


def normalize(block, norm_gain):
    values = block.astype(jnp.float32)
    inverse = lax.rsqrt(jnp.mean(values * values, axis=-1, keepdims=True) + epsilon)
    return (values * inverse * norm_gain).astype(jnp.bfloat16)


def shards(span_store, target, segment_ids, norm_gain, w_query, key_weight, value_weight):
    dp_count = lax.axis_size("dp")
    stored = span_store[0]
    tok_count = stored.shape[0]
    row_width = stored.shape[1]
    owners = target[0]
    onehot = (owners[:, None] == jnp.arange(dp_count, dtype=jnp.int32)[None, :]).astype(jnp.int32)
    ranking = jnp.cumsum(onehot, axis=0) - onehot
    slot_index = jnp.sum(ranking * onehot, axis=1)
    counts = jnp.sum(onehot, axis=0)
    capacity = tok_count // dp_count + tok_count // (2 * dp_count)
    outgoing = (
        jnp.zeros((dp_count, capacity, row_width), jnp.bfloat16).at[owners, slot_index].set(stored)
    )
    arrived, counts_wire = (
        lax.all_to_all(outgoing, "dp", split_axis=0, concat_axis=0, tiled=True),
        lax.all_to_all(counts.astype(jnp.bfloat16), "dp", split_axis=0, concat_axis=0, tiled=True),
    )
    got_counts = counts_wire.astype(jnp.int32)
    starts = jnp.cumsum(got_counts) - got_counts
    slot_ids = jnp.arange(capacity, dtype=jnp.int32)
    places = jnp.where(
        slot_ids[None, :] < got_counts[:, None], starts[:, None] + slot_ids[None, :], tok_count
    ).reshape(-1)
    placed = (
        jnp.zeros((tok_count, row_width), jnp.bfloat16)
        .at[places]
        .set(arrived.reshape(-1, row_width), mode="drop")
    )
    seg_all = segment_ids[0]
    length = seg_all.shape[0]
    query_cols = w_query.shape[1]
    key_cols = key_weight.shape[1]
    input_normed = lax.all_gather(normalize(placed, norm_gain), "seq", axis=0, tiled=True)
    pieces = (
        lax.all_gather(w_query, "dp", axis=0, tiled=True),
        lax.all_gather(key_weight, "dp", axis=0, tiled=True),
        lax.all_gather(value_weight, "dp", axis=0, tiled=True),
    )
    query_acc, key_acc, value_acc = tuple(
        (
            jnp.dot(input_normed, one_piece, preferred_element_type=jnp.float32)
            for one_piece in pieces
        )
    )
    groups = key_cols // HEAD_SIZE
    per_group = query_cols // key_cols
    key_pos = jnp.arange(length, dtype=jnp.int32)
    query_rows = (
        rotary_angles(query_acc.reshape(length, groups * per_group, HEAD_SIZE), key_pos)
        .astype(jnp.bfloat16)
        .reshape(length, groups, per_group, HEAD_SIZE)
    )
    key_matrix = rotary_angles(key_acc.reshape(length, groups, HEAD_SIZE), key_pos).astype(
        jnp.bfloat16
    )
    value_matrix = value_acc.astype(jnp.bfloat16).reshape(length, groups, HEAD_SIZE)
    scaling = HEAD_SIZE ** (-0.5)
    block_rows = min(512, length)
    scores = (
        jnp.einsum("qgrd,kgd->grqk", query_rows, key_matrix, preferred_element_type=jnp.float32)
        * scaling
    )
    allowed = (seg_all[:, None] == seg_all[None, :block_rows]) & (
        key_pos[None, :block_rows] <= key_pos[:, None]
    )
    exp_terms = jnp.where(allowed, jnp.exp(scores), 0.0)
    weights = (exp_terms / jnp.sum(exp_terms, axis=-1, keepdims=True)).astype(jnp.bfloat16)
    context = jnp.einsum(
        "grqk,kgd->qgrd", weights, value_matrix, preferred_element_type=jnp.float32
    )
    pieces_out = context.astype(jnp.bfloat16).reshape(block_rows, query_cols)
    returned = lax.all_to_all(pieces_out, "seq", split_axis=0, concat_axis=1, tiled=True)
    return returned[None]


def solution(mesh):
    placed = (
        P("dp", "seq", None),
        P("dp", "seq"),
        P("dp", None),
        P(),
        P("dp", "seq"),
        P("dp", "seq"),
        P("dp", "seq"),
    )
    return jax.shard_map(
        shards, mesh=mesh, in_specs=placed, out_specs=P("dp", "seq", None), check_vma=False
    )
```

profile of v0, /device:TPU:1, one launch (start us, length us, event | category | flops | bytes accessed | tf_op | source)
XLA Modules:
  0.0 389.7 jit_solution(1594310030817995858)
XLA Ops:
  6.5 0.7 all-gather.11.cloned.1.call-update
  7.3 0.7 fusion.24
  8.1 0.8 select_reduce_fusion
  8.9 0.7 copy.45
  9.7 11.9 %all-to-all-start = ((bf16[32,1,1]{2,1,0:T(2,128)(2,1)}), bf16[32,1,1]{2,1,0:T(2,128)(2,1)S(1)}, u32[]{:S(2)}, u32[]{:S(2)}) async-start(bf16[32,1,1]{2,1,0:T(2,128)(2,1)} %copy.45), calls=%async_computation | async-start | bytes 32768 | tf_op jit(solution)/shard_map/all_to_all | solution.py:44
  21.5 0.7 fusion.28
  22.3 23.9 %scatter_fusion = bf16[32,3,8192]{2,0,1:T(8,128)(2,1)S(1)} fusion(bf16[32,3,8192]{2,0,1:T(8,128)(2,1)S(1)} %broadcast_in_dim.21, s32[64]{0:T(128)S(1)} %fusion.28, bf16[64,8192]{1,0:T(8,128)(2,1)} %bitcast.80), kind=kCustom, calls=%fused_computation | custom fusion | bytes 3146240 | tf_op jit(solution)/shard_map/scatter | solution.py:40
  46.2 2.7 copy.47
  49.0 9.4 %all-to-all-start.1 = ((bf16[32,3,8192]{2,1,0:T(4,128)(2,1)}), bf16[32,3,8192]{2,1,0:T(4,128)(2,1)S(1)}, u32[]{:S(2)}, u32[]{:S(2)}) async-start(bf16[32,3,8192]{2,1,0:T(4,128)(2,1)} %copy.47), calls=%async_computation.1 | async-start | bytes 4194304 | tf_op jit(solution)/shard_map/all_to_all | solution.py:43
  59.5 62.1 %all-to-all-done.1 = bf16[32,3,8192]{2,1,0:T(4,128)(2,1)S(1)} async-done(((bf16[32,3,8192]{2,1,0:T(4,128)(2,1)}), bf16[32,3,8192]{2,1,0:T(4,128)(2,1)S(1)}, u32[]{:S(2)}, u32[]{:S(2)}) %all-to-all-start.1) | async-done | bytes 1572896 | tf_op jit(solution)/shard_map/all_to_all | solution.py:43
  121.7 2.6 reshape.239
  124.2 3.8 scatter_custom_fusion.1
  128.3 1.3 fusion.3
  129.7 0.7 all-gather.9.cloned.1.call-update
  131.8 15.4 %all-gather.11.cloned.1.call-done = bf16[8192,512]{1,0:T(8,128)(2,1)} async-done(((bf16[256,512]{1,0:T(8,128)(2,1)}), bf16[8192,512]{1,0:T(8,128)(2,1)}) %all-gather.11.cloned.1.call-update) | async-done | bytes 8388624 | tf_op jit(solution)/shard_map/all_gather | solution.py:63
  147.2 53.4 %all-gather.5.cloned.1.call-done = bf16[512,8192]{1,0:T(8,128)(2,1)} async-done(((bf16[64,8192]{1,0:T(8,128)(2,1)}), bf16[512,8192]{1,0:T(8,128)(2,1)}) %all-gather.5.cloned.1.call-update) | async-done | bytes 8388624 | tf_op jit(solution)/shard_map/all_gather | solution.py:61
  200.6 9.4 %fusion.33 = f32[512,512]{0,1:T(8,128)S(1)} fusion(bf16[512,8192]{1,0:T(8,128)(2,1)} %all-gather.5.cloned.1.call-done, bf16[8192,512]{1,0:T(8,128)(2,1)} %all-gather.11.cloned.1.call-done), kind=kOutput, calls=%fused_computation.62 | convolution fusion | flops 4294967296 | bytes 17825792 | tf_op jit(solution)/shard_map/dot_general | solution.py:69
  210.5 66.4 %all-gather.9.cloned.1.call-done = bf16[8192,128]{1,0:T(8,128)(2,1)} async-done(((bf16[256,128]{1,0:T(8,128)(2,1)}), bf16[8192,128]{1,0:T(8,128)(2,1)}) %all-gather.9.cloned.1.call-update) | async-done | bytes 2097168 | tf_op jit(solution)/shard_map/all_gather | solution.py:64
  276.9 6.8 %fusion.32 = f32[512,128]{0,1:T(8,128)S(1)} fusion(bf16[512,8192]{1,0:T(8,128)(2,1)} %all-gather.5.cloned.1.call-done, bf16[8192,128]{1,0:T(8,128)(2,1)} %all-gather.9.cloned.1.call-done), kind=kOutput, calls=%fused_computation.61 | convolution fusion | flops 1073741824 | bytes 10747904 | tf_op jit(solution)/shard_map/dot_general | solution.py:69
  283.8 3.1 fusion
  286.9 67.7 %all-gather.7.cloned.1.call-done = bf16[8192,128]{1,0:T(8,128)(2,1)} async-done(((bf16[256,128]{1,0:T(8,128)(2,1)}), bf16[8192,128]{1,0:T(8,128)(2,1)}) %all-gather.7.cloned.1.call-update) | async-done | bytes 2097168 | tf_op jit(solution)/shard_map/all_gather | solution.py:65
  354.5 8.8 %fusion.10 = bf16[512,1,4,128]{0,3,2,1:T(8,128)(2,1)S(1)} fusion(f32[4,512]{1,0:T(4,128)S(1)} %get-tuple-element.13, f32[512,512,4]{1,0,2:T(8,128)} %get-tuple-element.14, pred[512,512]{0,1:T(8,128)(4,1)S(1)} %fusion.15, bf16[512,8192]{1,0:T(8,128)(2,1)} %all-gather.5.cloned.1.call-done, bf16[8192,128]{1,0:T(8,128)(2,1)} %all-gather.7.cloned.1.call-done), kind=kOutput, calls=%fused_computation.14 | convolution fusion | flops 1346699264 | bytes 15474688 | tf_op jit(solution)/shard_map/grqk,kgd->qgrd/dot_general | solution.py:96
  363.9 18.0 %all_to_all.27 = bf16[8,64,512]{2,1,0:T(8,128)(2,1)S(1)} all-to-all(bf16[8,64,512]{2,1,0:T(8,128)(2,1)S(1)} %all_to_all.21), channel_id=1, replica_groups=mesh['dp'=32,'seq'=8] {'seq'}, dimensions={0} | all-to-all | bytes 1048576 | tf_op jit(solution)/shard_map/all_to_all | solution.py:100
  382.2 1.0 broadcast_in_dim.24
  (36 shorter events, 4.4 us)
Async XLA Ops:
  6.5 140.7 %all-gather.11.cloned.1.call-start = ((), (), s32[]{:S(2)}) async-start(), calls=%async_computation.6 | async-start | bytes 8650752 | tf_op jit(solution)/shard_map/all_gather | solution.py:63
  9.7 39.3 %all-to-all-start = ((bf16[32,1,1]{2,1,0:T(2,128)(2,1)}), bf16[32,1,1]{2,1,0:T(2,128)(2,1)S(1)}, u32[]{:S(2)}, u32[]{:S(2)}) async-start(bf16[32,1,1]{2,1,0:T(2,128)(2,1)} %copy.45), calls=%async_computation | async-start | bytes 32768 | tf_op jit(solution)/shard_map/all_to_all | solution.py:44
  49.0 79.4 %copy-start = (f32[8192]{0:T(1024)S(1)}, f32[8192]{0:T(1024)}, u32[]{:S(2)}) copy-start(f32[8192]{0:T(1024)} %param.10) | copy-start | bytes 98308
  49.0 72.7 %all-to-all-start.1 = ((bf16[32,3,8192]{2,1,0:T(4,128)(2,1)}), bf16[32,3,8192]{2,1,0:T(4,128)(2,1)S(1)}, u32[]{:S(2)}, u32[]{:S(2)}) async-start(bf16[32,3,8192]{2,1,0:T(4,128)(2,1)} %copy.47), calls=%async_computation.1 | async-start | bytes 4194304 | tf_op jit(solution)/shard_map/all_to_all | solution.py:43
  58.4 142.2 %all-gather.5.cloned.1.call-start = ((), (), s32[]{:S(2)}) async-start(), calls=%async_computation.3 | async-start | bytes 9437184 | tf_op jit(solution)/shard_map/all_gather | solution.py:61
  59.5 72.0 %copy-start.1 = (s32[1,512]{1,0:T(1,128)S(1)}, s32[1,512]{1,0:T(1,128)}, u32[]{:S(2)}) copy-start(s32[1,512]{1,0:T(1,128)} %param.9) | copy-start | bytes 6148
  129.6 147.3 %all-gather.9.cloned.1.call-start = ((), (), s32[]{:S(2)}) async-start(), calls=%async_computation.5 | async-start | bytes 2162688 | tf_op jit(solution)/shard_map/all_gather | solution.py:64
  130.4 224.2 %all-gather.7.cloned.1.call-start = ((), (), s32[]{:S(2)}) async-start(), calls=%async_computation.4 | async-start | bytes 2162688 | tf_op jit(solution)/shard_map/all_gather | solution.py:65
Sparse Core Ops, SparseCore 0:
  10.0 137.2 all-gather.10
  149.1 51.4 all-gather.4
  203.2 73.7 all-gather.8
  279.4 75.1 all-gather.6
where the time goes:
time: 390 us
  waiting for transfers between devices  267 us (68%)
  local copies, waits for them, and re-layouts  35.8 us (9%)
  matrix products  28.1 us (7%)
  starting transfers between devices  21.6 us (6%)
  blocking collectives  18 us (5%)
  between operations  13.3 us (3%)
  other arithmetic  6.2 us (2%)
    all_gather x1, waiting for transfers between devices, shards(): lax.all_gather(value_weight, 'dp', axis=0, tiled=True)  67.7 us
    all_gather x1, waiting for transfers between devices, shards(): lax.all_gather(key_weight, 'dp', axis=0, tiled=True)  66.4 us
    all_to_all x1, waiting for transfers between devices, shards(): lax.all_to_all(outgoing, 'dp', split_axis=0, concat_axis=0, tiled=True)  62.1 us
    all_gather x1, waiting for transfers between devices, shards(): lax.all_gather(normalize(placed, norm_gain), 'seq', axis=0, tiled=True)  53.4 us
    scatter x2, local copies, waits for them, and re-layouts, shards(): jnp.zeros((dp_count, capacity, row_width), jnp.bfloat16)  26.6 us
    all_to_all x1, blocking collectives, shards(): lax.all_to_all(pieces_out, 'seq', split_axis=0, concat_axis=1, tiled=True)  18 us
    dot_general x2, matrix products, shards(): jnp.dot(input_normed, one_piece, preferred_element_type=jnp.float32)  16.3 us
    all_gather x1, waiting for transfers between devices, shards(): lax.all_gather(w_query, 'dp', axis=0, tiled=True)  15.4 us
  transfers between devices with their start and end apart: 6, of which 5 were waited for; matrix products, arithmetic and copies ran while one was open for 15% of the time, Pallas kernels for 0%

commit v1 on v0

--- a/solution.py
+++ b/solution.py
@@ -6,6 +6,22 @@
 HEAD_SIZE = 128
 epsilon = 1e-05
 rope_base = 500000.0
+
+
+def ring_gather(x, axis, dim):
+    ways, here, turn = (lax.axis_size(axis), lax.axis_index(axis), x.shape[dim])
+    shape = [n * ways if d == dim else n for d, n in enumerate(x.shape)]
+    full = lax.dynamic_update_slice_in_dim(jnp.zeros(shape, x.dtype), x, here * turn, axis=dim)
+    going_up = going_down = x
+    for far in range(1, ways // 2 + 1):
+        going_up = lax.ppermute(going_up, axis, [(d, (d + 1) % ways) for d in range(ways)])
+        full = lax.dynamic_update_slice_in_dim(full, going_up, (here - far) % ways * turn, axis=dim)
+        if 2 * far < ways:
+            going_down = lax.ppermute(going_down, axis, [(d, (d - 1) % ways) for d in range(ways)])
+            full = lax.dynamic_update_slice_in_dim(
+                full, going_down, (here + far) % ways * turn, axis=dim
+            )
+    return full
 
 
 def rotary_angles(values, token_positions):
@@ -58,7 +74,7 @@
     length = seg_all.shape[0]
     query_cols = w_query.shape[1]
     key_cols = key_weight.shape[1]
-    input_normed = lax.all_gather(normalize(placed, norm_gain), "seq", axis=0, tiled=True)
+    input_normed = ring_gather(normalize(placed, norm_gain), "seq", 0)
     pieces = (
         lax.all_gather(w_query, "dp", axis=0, tiled=True),
         lax.all_gather(key_weight, "dp", axis=0, tiled=True),

time: 390 us -> 315 us (0.81)
  waiting for transfers between devices: 267 us -> 165 us
  local copies, waits for them, and re-layouts: 35.8 us -> 49 us
  starting transfers between devices: 21.6 us -> 32.8 us
    all_gather x1, waiting for transfers between devices: 66.4 us -> 0.01 us  [shards(): lax.all_gather(key_weight, 'dp', axis=0, tiled=True)]
    all_gather x1 -> x0, waiting for transfers between devices: 53.4 us -> none  [shards(): lax.all_gather(normalize(placed, norm_gain), 'seq', axis=0, tiled=True)]
    ppermute x0 -> x7, waiting for transfers between devices: none -> 37 us  [the longest x4 35.6 us: ring_gather(): lax.ppermute(going_up, axis, [(d, (d + 1) % ways) for d in range(ways)])]
    ppermute x0 -> x7, starting transfers between devices: none -> 11.6 us  [the longest x4 11 us: ring_gather(): lax.ppermute(going_up, axis, [(d, (d + 1) % ways) for d in range(ways)])]
    dynamic_update_slice x0 -> x7, local copies, waits for them, and re-layouts: none -> 7.44 us  [the longest x4 4.25 us: ring_gather(): lax.dynamic_update_slice_in_dim(full, going_up, (here - far) % ways * tur...]
    all_gather x1, waiting for transfers between devices: 67.7 us -> 60.3 us  [shards(): lax.all_gather(value_weight, 'dp', axis=0, tiled=True)]
    all_gather x1, waiting for transfers between devices: 15.4 us -> 9.1 us  [shards(): lax.all_gather(w_query, 'dp', axis=0, tiled=True)]
    all_to_all x1, waiting for transfers between devices: 62.1 us -> 57.4 us  [shards(): lax.all_to_all(outgoing, 'dp', split_axis=0, concat_axis=0, tiled=True)]
  transfers between devices with their start and end apart: 6 -> 12, of which waited for: 5 -> 10; matrix products, arithmetic and copies ran while one was open for 15% -> 23% of each run, Pallas kernels for 0% -> 0%
where the time goes in v1:
time: 315 us; the launch traced here: 314 us
  waiting for transfers between devices  165 us (52%)
  local copies, waits for them, and re-layouts  49 us (16%)
  starting transfers between devices  32.8 us (10%)
  matrix products  28.3 us (9%)
  blocking collectives  18 us (6%)
  between operations  13.5 us (4%)
  other arithmetic  7.66 us (2%)
    all_gather x1, waiting for transfers between devices, shards(): lax.all_gather(value_weight, 'dp', axis=0, tiled=True)  60.3 us
    all_to_all x1, waiting for transfers between devices, shards(): lax.all_to_all(outgoing, 'dp', split_axis=0, concat_axis=0, tiled=True)  57.4 us
    ppermute x4, waiting for transfers between devices, ring_gather(): lax.ppermute(going_up, axis, [(d, (d + 1) % ways) for d in range(ways)])  35.6 us
    scatter x2, local copies, waits for them, and re-layouts, shards(): jnp.zeros((dp_count, capacity, row_width), jnp.bfloat16)  26.6 us
    all_to_all x1, blocking collectives, shards(): lax.all_to_all(pieces_out, 'seq', split_axis=0, concat_axis=1, tiled=True)  18 us
    dot_general x2, matrix products, shards(): jnp.dot(input_normed, one_piece, preferred_element_type=jnp.float32)  16.4 us
    all_to_all x1, starting transfers between devices, shards(): lax.all_to_all(counts.astype(jnp.bfloat16), 'dp', split_axis=0, concat_ax...  11.9 us
    ppermute x4, starting transfers between devices, ring_gather(): lax.ppermute(going_up, axis, [(d, (d + 1) % ways) for d in range(ways)])  11 us
  transfers between devices with their start and end apart: 12, of which 10 were waited for; matrix products, arithmetic and copies ran while one was open for 23% of the time, Pallas kernels for 0%

profile of v1, /device:TPU:1, one launch (start us, length us, event | category | flops | bytes accessed | tf_op | source)
XLA Modules:
  0.0 314.4 jit_solution(15166218403769954020)
XLA Ops:
  10.4 11.9 %all-to-all-start = ((bf16[32,1,1]{2,1,0:T(2,128)(2,1)}), bf16[32,1,1]{2,1,0:T(2,128)(2,1)S(1)}, u32[]{:S(2)}, u32[]{:S(2)}) async-start(bf16[32,1,1]{2,1,0:T(2,128)(2,1)} %copy.45), calls=%async_computation | async-start | bytes 32768 | tf_op jit(solution)/shard_map/all_to_all | solution.py:60
  23.1 23.9 %scatter_fusion = bf16[32,3,8192]{2,0,1:T(8,128)(2,1)S(1)} fusion(bf16[32,3,8192]{2,0,1:T(8,128)(2,1)S(1)} %broadcast_in_dim.24, s32[64]{0:T(128)S(1)} %fusion.28, bf16[64,8192]{1,0:T(8,128)(2,1)} %bitcast.80), kind=kCustom, calls=%fused_computation | custom fusion | bytes 3146240 | tf_op jit(solution)/shard_map/scatter | solution.py:56
  47.0 2.7 copy.47
  49.7 9.3 %all-to-all-start.1 = ((bf16[32,3,8192]{2,1,0:T(4,128)(2,1)}), bf16[32,3,8192]{2,1,0:T(4,128)(2,1)S(1)}, u32[]{:S(2)}, u32[]{:S(2)}) async-start(bf16[32,3,8192]{2,1,0:T(4,128)(2,1)} %copy.47), calls=%async_computation.1 | async-start | bytes 4194304 | tf_op jit(solution)/shard_map/all_to_all | solution.py:59
  60.1 57.4 %all-to-all-done.1 = bf16[32,3,8192]{2,1,0:T(4,128)(2,1)S(1)} async-done(((bf16[32,3,8192]{2,1,0:T(4,128)(2,1)}), bf16[32,3,8192]{2,1,0:T(4,128)(2,1)S(1)}, u32[]{:S(2)}, u32[]{:S(2)}) %all-to-all-start.1) | async-done | bytes 1572896 | tf_op jit(solution)/shard_map/all_to_all | solution.py:59
  117.5 2.6 reshape.239
  120.1 4.0 %scatter_custom_fusion.1 = bf16[64,8192]{1,0:T(8,128)(2,1)S(1)} fusion(s32[96]{0:T(128)S(1)} %fusion.27, bf16[96,8192]{1,0:T(8,128)(2,1)} %reshape.239, bf16[]{:T(256)} %constant.70.clone.1), kind=kCustom, calls=%fused_computation.24 | custom fusion | bytes 1049088 | tf_op jit(solution)/shard_map/scatter | solution.py:71
  124.4 4.2 %broadcast_in_dim.20 = bf16[512,8192]{1,0:T(8,128)(2,1)} broadcast(bf16[]{:T(256)} %constant.70.clone.1), dimensions={} | broadcast | bytes 8388610 | tf_op jit(solution)/shard_map/broadcast_in_dim | solution.py:14
  128.7 1.3 constant_dynamic-update-slice_fusion.7
  130.0 3.5 %collective-permute-start = (bf16[64,8192]{1,0:T(8,128)(2,1)S(1)}, bf16[64,8192]{1,0:T(8,128)(2,1)S(1)}, u32[]{:S(2)}, u32[]{:S(2)}) collective-permute-start(bf16[64,8192]{1,0:T(8,128)(2,1)S(1)} %get-tuple-element.8), channel_id=1, source_target_pairs={{0,1},{1,2},{2,3},{3,4},{4,5},{5,6},{6,7},{7,0},{8,9},{9,10},{10,1... | collective-permute-start | bytes 3145736 | tf_op jit(solution)/shard_map/ppermute | solution.py:17
  136.6 8.7 %collective-permute-done = bf16[64,8192]{1,0:T(8,128)(2,1)S(1)} collective-permute-done((bf16[64,8192]{1,0:T(8,128)(2,1)S(1)}, bf16[64,8192]{1,0:T(8,128)(2,1)S(1)}, u32[]{:S(2)}, u32[]{:S(2)}) %collective-permute-start) | collective-permute-done | bytes 1048608 | tf_op jit(solution)/shard_map/ppermute | solution.py:17
  145.3 2.5 collective-permute-start.2
  150.3 9.2 %collective-permute-done.2 = bf16[64,8192]{1,0:T(8,128)(2,1)S(1)} collective-permute-done((bf16[64,8192]{1,0:T(8,128)(2,1)S(1)}, bf16[64,8192]{1,0:T(8,128)(2,1)S(1)}, u32[]{:S(2)}, u32[]{:S(2)}) %collective-permute-start.2) | collective-permute-done | bytes 1048608 | tf_op jit(solution)/shard_map/ppermute | solution.py:17
  159.5 2.5 collective-permute-start.4
  165.4 8.3 %collective-permute-done.4 = bf16[64,8192]{1,0:T(8,128)(2,1)S(1)} collective-permute-done((bf16[64,8192]{1,0:T(8,128)(2,1)S(1)}, bf16[64,8192]{1,0:T(8,128)(2,1)S(1)}, u32[]{:S(2)}, u32[]{:S(2)}) %collective-permute-start.4) | collective-permute-done | bytes 1048608 | tf_op jit(solution)/shard_map/ppermute | solution.py:17
  173.7 2.5 collective-permute-start.6
  178.5 9.4 %collective-permute-done.6 = bf16[64,8192]{1,0:T(8,128)(2,1)S(1)} collective-permute-done((bf16[64,8192]{1,0:T(8,128)(2,1)S(1)}, bf16[64,8192]{1,0:T(8,128)(2,1)S(1)}, u32[]{:S(2)}, u32[]{:S(2)}) %collective-permute-start.6) | collective-permute-done | bytes 1048608 | tf_op jit(solution)/shard_map/ppermute | solution.py:17
  189.0 7.0 %fusion.33 = f32[512,128]{0,1:T(8,128)S(1)} fusion(bf16[512,8192]{1,0:T(8,128)(2,1)} %constant_dynamic-update-slice_fusion, bf16[8192,128]{1,0:T(8,128)(2,1)} %all-gather.6.cloned.1.call-done), kind=kOutput, calls=%fused_computation.69 | convolution fusion | flops 1073741824 | bytes 10747904 | tf_op jit(solution)/shard_map/dot_general | solution.py:85
  196.0 9.1 %all-gather.8.cloned.1.call-done = bf16[8192,512]{1,0:T(8,128)(2,1)} async-done(((bf16[256,512]{1,0:T(8,128)(2,1)}), bf16[8192,512]{1,0:T(8,128)(2,1)}) %all-gather.8.cloned.1.call-update) | async-done | bytes 8388624 | tf_op jit(solution)/shard_map/all_gather | solution.py:79
  205.1 9.4 %fusion.34 = f32[512,512]{0,1:T(8,128)S(1)} fusion(bf16[512,8192]{1,0:T(8,128)(2,1)} %constant_dynamic-update-slice_fusion, bf16[8192,512]{1,0:T(8,128)(2,1)} %all-gather.8.cloned.1.call-done), kind=kOutput, calls=%fused_computation.70 | convolution fusion | flops 4294967296 | bytes 17825792 | tf_op jit(solution)/shard_map/dot_general | solution.py:85
  215.8 3.1 fusion
  218.9 60.3 %all-gather.4.cloned.1.call-done = bf16[8192,128]{1,0:T(8,128)(2,1)} async-done(((bf16[256,128]{1,0:T(8,128)(2,1)}), bf16[8192,128]{1,0:T(8,128)(2,1)}) %all-gather.4.cloned.1.call-update) | async-done | bytes 2097168 | tf_op jit(solution)/shard_map/all_gather | solution.py:81
  279.2 8.8 %fusion.10 = bf16[512,1,4,128]{0,3,2,1:T(8,128)(2,1)S(1)} fusion(f32[4,512]{1,0:T(4,128)S(1)} %get-tuple-element.15, f32[512,512,4]{1,0,2:T(8,128)} %get-tuple-element.16, pred[512,512]{0,1:T(8,128)(4,1)S(1)} %copy-done.3, bf16[512,8192]{1,0:T(8,128)(2,1)} %constant_dynamic-update-slice_fusion, bf16[8192,128]{1,0:T(8,128)(2,1)} %all-gather.4.cloned.1.call-done), kind=kOutput, calls=%fused_computation.14 | convolution fusion | flops 1346699264 | bytes 15474688 | tf_op jit(solution)/shard_map/grqk,kgd->qgrd/dot_general | solution.py:112
  288.5 18.0 %all_to_all.27 = bf16[8,64,512]{2,1,0:T(8,128)(2,1)S(1)} all-to-all(bf16[8,64,512]{2,1,0:T(8,128)(2,1)S(1)} %all_to_all.21), channel_id=1, replica_groups=mesh['dp'=32,'seq'=8] {'seq'}, dimensions={0} | all-to-all | bytes 1048576 | tf_op jit(solution)/shard_map/all_to_all | solution.py:116
  (64 shorter events, 21.3 us)
Async XLA Ops:
  6.5 182.5 %all-gather.6.cloned.1.call-start = ((), (), s32[]{:S(2)}) async-start(), calls=%async_computation.4 | async-start | bytes 2162688 | tf_op jit(solution)/shard_map/all_gather | solution.py:80
  7.3 197.8 %all-gather.8.cloned.1.call-start = ((), (), s32[]{:S(2)}) async-start(), calls=%async_computation.5 | async-start | bytes 8650752 | tf_op jit(solution)/shard_map/all_gather | solution.py:79
  10.4 39.3 %all-to-all-start = ((bf16[32,1,1]{2,1,0:T(2,128)(2,1)}), bf16[32,1,1]{2,1,0:T(2,128)(2,1)S(1)}, u32[]{:S(2)}, u32[]{:S(2)}) async-start(bf16[32,1,1]{2,1,0:T(2,128)(2,1)} %copy.45), calls=%async_computation | async-start | bytes 32768 | tf_op jit(solution)/shard_map/all_to_all | solution.py:60
  49.7 67.8 %all-to-all-start.1 = ((bf16[32,3,8192]{2,1,0:T(4,128)(2,1)}), bf16[32,3,8192]{2,1,0:T(4,128)(2,1)S(1)}, u32[]{:S(2)}, u32[]{:S(2)}) async-start(bf16[32,3,8192]{2,1,0:T(4,128)(2,1)} %copy.47), calls=%async_computation.1 | async-start | bytes 4194304 | tf_op jit(solution)/shard_map/all_to_all | solution.py:59
  59.0 220.2 %all-gather.4.cloned.1.call-start = ((), (), s32[]{:S(2)}) async-start(), calls=%async_computation.3 | async-start | bytes 2162688 | tf_op jit(solution)/shard_map/all_gather | solution.py:81
  124.4 4.2 %copy-start.4 = (f32[8192]{0:T(1024)S(1)}, f32[8192]{0:T(1024)}, u32[]{:S(2)}) copy-start(f32[8192]{0:T(1024)} %param.10) | copy-start | bytes 98308
  128.7 7.0 %copy-start.5 = (s32[1,512]{1,0:T(1,128)S(1)}, s32[1,512]{1,0:T(1,128)}, u32[]{:S(2)}) copy-start(s32[1,512]{1,0:T(1,128)} %param.9) | copy-start | bytes 6148
  130.0 15.3 %collective-permute-start = (bf16[64,8192]{1,0:T(8,128)(2,1)S(1)}, bf16[64,8192]{1,0:T(8,128)(2,1)S(1)}, u32[]{:S(2)}, u32[]{:S(2)}) collective-permute-start(bf16[64,8192]{1,0:T(8,128)(2,1)S(1)} %get-tuple-element.8), channel_id=1, source_target_pairs={{0,1},{1,2},{2,3},{3,4},{4,5},{5,6},{6,7},{7,0},{8,9},{9,10},{10,1... | collective-permute-start | bytes 3145736 | tf_op jit(solution)/shard_map/ppermute | solution.py:17
  133.5 14.6 %collective-permute-start.1 = (bf16[64,8192]{1,0:T(8,128)(2,1)S(1)}, bf16[64,8192]{1,0:T(8,128)(2,1)S(1)}, u32[]{:S(2)}, u32[]{:S(2)}) collective-permute-start(bf16[64,8192]{1,0:T(8,128)(2,1)S(1)} %get-tuple-element.8), channel_id=1, source_target_pairs={{0,7},{1,0},{2,1},{3,2},{4,3},{5,4},{6,5},{7,6},{8,15},{9,8},{10,9... | collective-permute-start | bytes 3145736 | tf_op jit(solution)/shard_map/ppermute | solution.py:20
  134.2 0.6 copy-start.1
  145.3 14.2 %collective-permute-start.2 = (bf16[64,8192]{1,0:T(8,128)(2,1)S(1)}, bf16[64,8192]{1,0:T(8,128)(2,1)S(1)}, u32[]{:S(2)}, u32[]{:S(2)}) collective-permute-start(bf16[64,8192]{1,0:T(8,128)(2,1)S(1)} %collective-permute-done), channel_id=1, source_target_pairs={{0,1},{1,2},{2,3},{3,4},{4,5},{5,6},{6,7},{7,0},{8,9},{9,10},{10,1... | collective-permute-start | bytes 3145736 | tf_op jit(solution)/shard_map/ppermute | solution.py:17
  148.2 14.6 %collective-permute-start.3 = (bf16[64,8192]{1,0:T(8,128)(2,1)S(1)}, bf16[64,8192]{1,0:T(8,128)(2,1)S(1)}, u32[]{:S(2)}, u32[]{:S(2)}) collective-permute-start(bf16[64,8192]{1,0:T(8,128)(2,1)S(1)} %collective-permute-done.1), channel_id=1, source_target_pairs={{0,7},{1,0},{2,1},{3,2},{4,3},{5,4},{6,5},{7,6},{8,15},{9,8},{10,9... | collective-permute-start | bytes 3145736 | tf_op jit(solution)/shard_map/ppermute | solution.py:20
  159.5 14.2 %collective-permute-start.4 = (bf16[64,8192]{1,0:T(8,128)(2,1)S(1)}, bf16[64,8192]{1,0:T(8,128)(2,1)S(1)}, u32[]{:S(2)}, u32[]{:S(2)}) collective-permute-start(bf16[64,8192]{1,0:T(8,128)(2,1)S(1)} %collective-permute-done.2), channel_id=1, source_target_pairs={{0,1},{1,2},{2,3},{3,4},{4,5},{5,6},{6,7},{7,0},{8,9},{9,10},{10,1... | collective-permute-start | bytes 3145736 | tf_op jit(solution)/shard_map/ppermute | solution.py:17
  162.8 14.6 %collective-permute-start.5 = (bf16[64,8192]{1,0:T(8,128)(2,1)S(1)}, bf16[64,8192]{1,0:T(8,128)(2,1)S(1)}, u32[]{:S(2)}, u32[]{:S(2)}) collective-permute-start(bf16[64,8192]{1,0:T(8,128)(2,1)S(1)} %collective-permute-done.3), channel_id=1, source_target_pairs={{0,7},{1,0},{2,1},{3,2},{4,3},{5,4},{6,5},{7,6},{8,15},{9,8},{10,9... | collective-permute-start | bytes 3145736 | tf_op jit(solution)/shard_map/ppermute | solution.py:20
  173.7 14.2 %collective-permute-start.6 = (bf16[64,8192]{1,0:T(8,128)(2,1)S(1)}, bf16[64,8192]{1,0:T(8,128)(2,1)S(1)}, u32[]{:S(2)}, u32[]{:S(2)}) collective-permute-start(bf16[64,8192]{1,0:T(8,128)(2,1)S(1)} %collective-permute-done.4), channel_id=1, source_target_pairs={{0,1},{1,2},{2,3},{3,4},{4,5},{5,6},{6,7},{7,0},{8,9},{9,10},{10,1... | collective-permute-start | bytes 3145736 | tf_op jit(solution)/shard_map/ppermute | solution.py:17
  214.5 1.0 copy-start
  214.5 1.2 copy-start.2
  214.6 1.2 copy-start.3
Sparse Core Ops, SparseCore 0:
  9.9 93.8 all-gather.5
  106.4 98.6 all-gather.7
  207.7 71.4 all-gather.3
